TPU v7x, 32 devices: a whole 2x2x4 slice. The times are simulated.
32 devices in a mesh: groups: 2 (over x), rows: 4 (over y, core), cols: 4 (over z).
Axes of the slice: x: 2, y: 2, z: 4, core: 2. Of those that a mesh axis runs over, the one named last changes fastest.
Arguments:
- tokens: bfloat16 [128, 32, 512], P(('groups', 'rows'), 'cols'), parts along dimension 0, may hold values from -6 to 6
- top_state: bfloat16 [64, 16, 2048], P(('groups', 'cols')), parts along dimension 0, may hold values from -4 to 4
- in_weight: bfloat16 [512, 1024], replicated, may hold values from -0.25 to 0.25
- conv_weight: float32 [9, 512], replicated, may hold values from -2 to 2
- bc_weight: bfloat16 [512, 256], replicated, may hold values from -0.25 to 0.25
- step_weight: bfloat16 [512, 32], replicated, may hold values from -0.25 to 0.25
- step_bias: float32 [32], replicated, may hold values from -2 to 0.5
- across_rate: float32 [16], replicated, may hold values from 0.03125 to 0.3
- down_rate: float32 [16], replicated, may hold values from 0.015625 to 0.3
- skip_gain: float32 [16], replicated, may hold values from 0.5 to 1.5
- norm_gain: float32 [512], replicated, may hold values from 0.1 to 1.9
- out_weight: bfloat16 [512, 512], replicated, may hold values from -0.25 to 0.25
Outputs:
- layer_out: bfloat16 [128, 32, 512], P(('groups', 'rows'), 'cols'), parts along dimension 0
There are 2 independent parts, one for each index of `groups`. A program takes and returns all parts, laid end to end along the dimension named above; an argument that names none is the same for every part. Nothing has to cross between parts.
All inputs are finite; a program needn't handle non-finite values.
Results may differ from a plain program's by a relative error of at most 0.0095.
Values may be sent and summed in bfloat16 or wider, within the bound.
A program may use at most 128 MiB of HBM per device.

v0:
```python
import jax
import jax.numpy as jnp
from jax import lax
from jax.sharding import PartitionSpec as P


def with_halo(block, sides, width):
    for axis, dim in sides:
        count = lax.axis_size(axis)
        forward = [(i, i + 1) for i in range(count - 1)]
        backward = [(target, source) for source, target in forward]
        low = lax.ppermute(
            lax.slice_in_dim(block, block.shape[dim] - width, None, axis=dim), axis, forward
        )
        high = lax.ppermute(lax.slice_in_dim(block, 0, width, axis=dim), axis, backward)
        block = jnp.concatenate([low, block, high], axis=dim)
    return block


def from_behind(array, axis, by):
    size = lax.axis_size(axis)
    pairs = [(i, i + by) for i in range(size) if 0 <= i + by < size]
    return lax.ppermute(array, axis, pairs)


def carried_in(value, axis, join, neutral):
    count, mine = (lax.axis_size(axis), lax.axis_index(axis))
    pieces = jax.tree.map(lambda part: lax.all_gather(part, axis), value)
    subtotal = jax.tree.map(
        lambda part, zero: jnp.full_like(part, 0) + jnp.asarray(zero, part.dtype), value, neutral
    )

    def hop(position, subtotal):
        longer = join(subtotal, jax.tree.map(lambda part: part[position], pieces))
        return jax.tree.map(lambda new, old: jnp.where(position < mine, new, old), longer, subtotal)

    return lax.fori_loop(0, count - 1, hop, subtotal)


def block_sweep(values, b_in, c_in, steps, log_decay):
    cumulative = jnp.cumsum(log_decay, axis=1)
    length = log_decay.shape[1]
    lower = (jnp.arange(length)[:, None] >= jnp.arange(length)[None, :])[None, :, :, None]
    differ = cumulative[:, :, None, :] - cumulative[:, None, :, :]
    weights = jnp.where(lower, jnp.exp(jnp.where(lower, differ, 0.0)), 0.0)
    scores = jnp.einsum("ain,ajn->aij", c_in, b_in, precision=lax.Precision.HIGHEST)
    mixing = weights * scores[..., None] * steps[:, None, :, :]
    local = jnp.einsum("aijk,ajkp->aikp", mixing, values, precision=lax.Precision.HIGHEST)
    tail = jnp.exp(cumulative[:, -1:, :] - cumulative) * steps
    ending = jnp.einsum("ajk,ajkp,ajn->akpn", tail, values, b_in, precision=lax.Precision.HIGHEST)
    return (local, ending, jnp.exp(cumulative[:, -1, :]), jnp.exp(cumulative))


def carried(c_in, growth, entering):
    return (
        jnp.einsum("ain,akpn->aikp", c_in, entering, precision=lax.Precision.HIGHEST)
        * growth[..., None]
    )


def compose(earlier, later):
    return (earlier[0] * later[0], earlier[1] * later[0][..., None] + later[1])


def shards(
    tokens,
    top_state,
    in_weight,
    conv_weight,
    bc_weight,
    step_weight,
    step_bias,
    across_rate,
    down_rate,
    skip_gain,
    norm_gain,
    out_weight,
):
    rows_dev, cols_dev, model_width = tokens.shape
    inner_width = out_weight.shape[0]
    head_count = across_rate.shape[0]
    head_width = inner_width // head_count
    state_width = bc_weight.shape[1] // 4
    flat_width = head_width * state_width
    projected = jnp.dot(
        tokens.reshape(-1, model_width), in_weight, preferred_element_type=jnp.float32
    )
    projected = projected.reshape(rows_dev, cols_dev, 2 * inner_width)
    mixer_in = projected[..., :inner_width].astype(jnp.bfloat16)
    gate_in = projected[..., inner_width:].astype(jnp.bfloat16)
    padded = with_halo(mixer_in, (("rows", 0), ("cols", 1)), 1).astype(jnp.float32)
    summed = jnp.zeros((rows_dev, cols_dev, inner_width), jnp.float32)
    for row_off in range(3):
        for col_off in range(3):
            summed = (
                summed
                + conv_weight[3 * row_off + col_off]
                * padded[row_off : row_off + rows_dev, col_off : col_off + cols_dev]
            )
    values_low = jax.nn.silu(summed).astype(jnp.bfloat16)
    flat = values_low.reshape(-1, inner_width)
    maps = jnp.dot(flat, bc_weight, preferred_element_type=jnp.float32).reshape(
        rows_dev, cols_dev, 4 * state_width
    )
    steps = jax.nn.softplus(
        jnp.dot(flat, step_weight, preferred_element_type=jnp.float32) + step_bias
    )
    steps = steps.reshape(rows_dev, cols_dev, 2 * head_count)
    values = values_low.astype(jnp.float32).reshape(rows_dev, cols_dev, head_count, head_width)
    step_across = steps[..., :head_count]
    step_down = steps[..., head_count:]
    b_across = maps[..., :state_width]
    c_across = maps[..., state_width : 2 * state_width]
    b_down = maps[..., 2 * state_width : 3 * state_width]
    c_down = maps[..., 3 * state_width :]
    local_across, end_across, total_across, growth_across = block_sweep(
        values, b_across, c_across, step_across, -step_across * across_rate
    )
    end_across = end_across.reshape(rows_dev, head_count, flat_width)

    def advance_across(turn, pair):
        leaving = pair[1]
        entering = from_behind(leaving, "cols", 1)
        return (entering, total_across[..., None] * entering + end_across)

    entering_across, leaving_across = lax.fori_loop(
        0, lax.axis_size("cols") - 1, advance_across, (jnp.zeros_like(end_across), end_across)
    )
    entering_across = entering_across.reshape(rows_dev, head_count, head_width, state_width)
    y_across = local_across + carried(c_across, growth_across, entering_across)
    values_t = jnp.swapaxes(values, 0, 1)
    step_t = jnp.swapaxes(step_down, 0, 1)
    b_down_t = jnp.swapaxes(b_down, 0, 1)
    c_down_t = jnp.swapaxes(c_down, 0, 1)
    top_values = top_state.astype(jnp.float32)
    local_down, end_down, total_down, growth_down = block_sweep(
        values_t, b_down_t, c_down_t, step_t, -step_t * down_rate
    )
    end_down = end_down.reshape(cols_dev, head_count, flat_width)
    identity = (jnp.ones_like(total_down), jnp.zeros_like(end_down))
    before_down, prefix_down = carried_in((total_down, end_down), "rows", compose, identity)
    entering_down = prefix_down + before_down[..., None] * top_values
    entering_down = entering_down.reshape(cols_dev, head_count, head_width, state_width)
    y_down = jnp.swapaxes(local_down + carried(c_down_t, growth_down, entering_down), 0, 1)
    mixed = y_across + y_down + skip_gain[:, None] * values
    gated = mixed.reshape(rows_dev, cols_dev, inner_width) * jax.nn.silu(
        gate_in.astype(jnp.float32)
    )
    scale = lax.rsqrt(jnp.mean(gated * gated, axis=-1, keepdims=True) + 1e-05)
    normed = (gated * scale * norm_gain).astype(jnp.bfloat16)
    result = jnp.dot(
        normed.reshape(-1, inner_width), out_weight, preferred_element_type=jnp.float32
    )
    return result.astype(jnp.bfloat16).reshape(rows_dev, cols_dev, model_width)


def solution(mesh):
    in_specs = (
        P(("groups", "rows"), "cols", None),
        P(("groups", "cols"), None, None),
        P(),
        P(),
        P(),
        P(),
        P(),
        P(),
        P(),
        P(),
        P(),
        P(),
    )
    out_specs = P(("groups", "rows"), "cols", None)
    return jax.shard_map(shards, mesh=mesh, in_specs=in_specs, out_specs=out_specs, check_vma=False)
```

profile of v0, /device:TPU:25, one launch (start us, length us, event | category | flops | bytes accessed | tf_op | source)
XLA Modules:
  0.0 268.9 jit_solution(3467850956297400062)
XLA Ops:
  6.5 1.2 copy-done
  7.8 1.2 convolution_convert_fusion
  9.0 2.6 collective-permute-start.2
  11.6 3.0 %collective-permute-start.1 = (bf16[1,8,512]{2,1,0:T(8,128)(2,1)S(1)}, bf16[1,8,512]{2,1,0:T(8,128)(2,1)S(1)}, u32[]{:S(2)}, u32[]{:S(2)}) collective-permute-start(bf16[1,8,512]{2,1,0:T(8,128)(2,1)S(1)} %get-tuple-element.189), channel_id=1, source_target_pairs={{0,4},{4,8},{8,12},{1,5},{5,9},{9,13},{2,6},{6,10},{10,14},{3,7},{... | collective-permute-start | bytes 24584 | tf_op jit(solution)/shard_map/ppermute | solution.py:12
  14.7 0.7 collective-permute-done.1
  15.5 2.1 collective-permute-start.4
  17.6 1.3 collective-permute-start.3
  18.9 1.0 fusion.88
  19.9 2.9 %collective-permute-done.3 = bf16[18,1,512]{2,1,0:T(2,128)(2,1)S(1)} collective-permute-done((bf16[18,1,512]{2,1,0:T(2,128)(2,1)S(1)}, bf16[18,1,512]{2,1,0:T(2,128)(2,1)S(1)}, u32[]{:S(2)}, u32[]{:S(2)}) %collective-permute-start.3) | collective-permute-done | bytes 18464 | tf_op jit(solution)/shard_map/ppermute | solution.py:12
  23.2 1.1 reshape.111
  24.9 0.6 exponential_bitcast_fusion
  25.6 0.7 slice_bitcast_fusion.4
  26.3 4.8 %fusion.8 = f32[8,16,32,64]{3,2,1,0:T(8,128)S(1)} fusion(f32[8,16,16]{1,2,0:T(8,128)S(1)} %copy.67, bf16[16,8,16,32]{3,2,1,0:T(8,128)(2,1)} %reshape.111, f32[8,16,64,1]{2,0,1,3:T(8,128)S(1)} %get-tuple-element.195), kind=kOutput, calls=%fused_computation.21 | convolution fusion | flops 50462720 | bytes 1220608 | tf_op jit(solution)/shard_map/ajk,ajkp,ajn->akpn/dot_general | solution.py:50
  31.1 1.6 all_gather_reshape.3
  32.8 0.6 iota_compare_fusion.1
  33.4 0.6 iota_compare_fusion
  34.0 0.7 copy.61
  34.7 0.7 fusion.86
  35.6 0.8 copy.53
  36.3 0.7 fusion.87
  37.1 8.7 %fusion.5 = f32[16,16,32,64]{3,2,1,0:T(8,128)} fusion(f32[16,8,16]{1,2,0:T(8,128)S(1)} %copy.57, bf16[16,8,16,32]{3,2,1,0:T(8,128)(2,1)S(1)} %copy-done.2, f32[16,8,256]{2,1,0:T(8,128)S(1)} %fusion.56), kind=kOutput, calls=%fused_computation.16 | convolution fusion | flops 50462720 | bytes 2818048 | tf_op jit(solution)/shard_map/ajk,ajkp,ajn->akpn/dot_general | solution.py:50
  45.7 3.6 %reshape.114 = f32[16,16,2048]{2,1,0:T(8,128)S(1)} reshape(f32[16,16,32,64]{3,2,1,0:T(8,128)} %fusion.5) | data formatting | bytes 4194304 | tf_op jit(solution)/shard_map/reshape | solution.py:119
  49.3 1.3 copy.107
  50.6 153.2 %while.28 = (s32[]{:T(128)}, f32[16,16,2048]{2,1,0:T(8,128)}, f32[16,16,2048]{2,1,0:T(8,128)}, f32[16,16]{1,0:T(8,128)S(1)}, f32[16,16,2048]{2,1,0:T(8,128)S(1)}, /*index=5*/s32[]{:T(128)}) while((s32[]{:T(128)}, f32[16,16,2048]{2,1,0:T(8,128)}, f32[16,16,2048]{2,1,0:T(8,128)}, f32[16,16]{1,0:T(8,128)S(1)}, f32[16,16,2048]{2,1,0:T(8,128)S(1)}, ...), condition=%wide.region_2.3_spmd, body=%wide.region_1.2_spmd.sunk | while | flops 1048578 | bytes 14681197 | solution.py:126
  50.6 1.3 collective-permute-start
  51.9 47.6 %collective-permute-done = f32[16,16,2048]{2,1,0:T(8,128)} collective-permute-done((f32[16,16,2048]{2,1,0:T(8,128)}, f32[16,16,2048]{2,1,0:T(8,128)}, u32[]{:S(2)}, u32[]{:S(2)}) %collective-permute-start) | collective-permute-done | bytes 2097184 | tf_op jit(solution)/shard_map/while/body/eval_jaxpr/ppermute | solution.py:23
  99.5 3.2 %multiply_add_fusion.3 = f32[16,16,2048]{2,1,0:T(8,128)} fusion(f32[16,16,2048]{2,1,0:T(8,128)S(1)} %get-tuple-element.301, f32[16,16,2048]{2,1,0:T(8,128)} %collective-permute-done, f32[16,16]{1,0:T(8,128)S(1)} %get-tuple-element.300), kind=kLoop, calls=%fused_computation.clone.1 | loop fusion | flops 1048576 | bytes 6292480 | tf_op jit(solution)/shard_map/while/body/eval_jaxpr/add | solution.py:124
  102.6 1.3 collective-permute-start
  103.9 46.6 %collective-permute-done = f32[16,16,2048]{2,1,0:T(8,128)} collective-permute-done((f32[16,16,2048]{2,1,0:T(8,128)}, f32[16,16,2048]{2,1,0:T(8,128)}, u32[]{:S(2)}, u32[]{:S(2)}) %collective-permute-start) | collective-permute-done | bytes 2097184 | tf_op jit(solution)/shard_map/while/body/eval_jaxpr/ppermute | solution.py:23
  150.6 3.2 %multiply_add_fusion.3 = f32[16,16,2048]{2,1,0:T(8,128)} fusion(f32[16,16,2048]{2,1,0:T(8,128)S(1)} %get-tuple-element.301, f32[16,16,2048]{2,1,0:T(8,128)} %collective-permute-done, f32[16,16]{1,0:T(8,128)S(1)} %get-tuple-element.300), kind=kLoop, calls=%fused_computation.clone.1 | loop fusion | flops 1048576 | bytes 6292480 | tf_op jit(solution)/shard_map/while/body/eval_jaxpr/add | solution.py:124
  153.7 1.3 collective-permute-start
  155.0 45.7 %collective-permute-done = f32[16,16,2048]{2,1,0:T(8,128)} collective-permute-done((f32[16,16,2048]{2,1,0:T(8,128)}, f32[16,16,2048]{2,1,0:T(8,128)}, u32[]{:S(2)}, u32[]{:S(2)}) %collective-permute-start) | collective-permute-done | bytes 2097184 | tf_op jit(solution)/shard_map/while/body/eval_jaxpr/ppermute | solution.py:23
  200.7 3.2 %multiply_add_fusion.3 = f32[16,16,2048]{2,1,0:T(8,128)} fusion(f32[16,16,2048]{2,1,0:T(8,128)S(1)} %get-tuple-element.301, f32[16,16,2048]{2,1,0:T(8,128)} %collective-permute-done, f32[16,16]{1,0:T(8,128)S(1)} %get-tuple-element.300), kind=kLoop, calls=%fused_computation.clone.1 | loop fusion | flops 1048576 | bytes 6292480 | tf_op jit(solution)/shard_map/while/body/eval_jaxpr/add | solution.py:124
  203.9 4.9 %reshape.115 = f32[16,16,32,64]{3,2,1,0:T(8,128)} reshape(f32[16,16,2048]{2,1,0:T(8,128)} %get-tuple-element.141) | data formatting | bytes 4194304 | tf_op jit(solution)/shard_map/reshape | solution.py:129
  209.1 0.8 copy.71
  209.8 0.8 copy.55
  210.6 8.4 %all-gather = f32[32,1,16]{2,0,1:T(8,128)S(1)} all-gather(f32[8,1,16]{2,0,1:T(8,128)S(1)} %get-tuple-element.203), channel_id=2, replica_groups=mesh['groups'=2,'rows'=4,'cols'=4] {'rows'}, dimensions={0}, use_global_device_ids=true | all-gather | bytes 2560 | tf_op jit(solution)/shard_map/all_gather | solution.py:28
  219.6 2.1 fusion.11
  221.7 19.6 %convolution_multiply_fusion = f32[16,8,16,32]{3,1,2,0:T(8,128)} fusion(f32[16,16,32,64]{3,2,1,0:T(8,128)} %reshape.115, f32[16,8,16]{1,2,0:T(8,128)S(1)} %copy.59, f32[16,8,256]{2,1,0:T(8,128)S(1)} %fusion.56), kind=kOutput, calls=%fused_computation.5 | convolution fusion | flops 50397184 | bytes 2555904 | tf_op jit(solution)/shard_map/ain,akpn->aikp/dot_general | solution.py:56
  241.3 4.6 %while.29 = (s32[]{:T(128)}, f32[8,16]{1,0:T(8,128)S(1)}, f32[8,16,2048]{2,1,0:T(8,128)S(1)}, s32[]{:T(128)}, f32[4,8,16]{2,1,0:T(8,128)S(1)}, /*index=5*/f32[4,8,16,2048]{3,2,1,0:T(8,128)}, s32[]{:T(128)}, s32[]{:T(128)}) while((s32[]{:T(128)}, f32[8,16]{1,0:T(8,128)S(1)}, f32[8,16,2048]{2,1,0:T(8,128)S(1)}, s32[]{:T(128)}, ...), condition=%wide.region_5.6_spmd.clone, body=%wide.region_4.5_spmd.clone.sunk | while | flops 1048964 | bytes 3148411 | solution.py:37
  241.4 1.5 fusion.96
  242.9 1.5 fusion.96
  244.4 1.5 fusion.96
  245.9 1.2 multiply_add_fusion.1
  247.1 2.0 reshape.116
  249.2 8.2 %fusion.66 = f32[8,16,16,32]{3,1,2,0:T(8,128)S(1)} fusion(f32[8,16,32,64]{3,2,1,0:T(8,128)S(1)} %reshape.116, f32[8,16,64,1]{2,0,1,3:T(8,128)S(1)} %get-tuple-element.194), kind=kOutput, calls=%fused_computation.94 | convolution fusion | flops 50331648 | bytes 1343488 | tf_op jit(solution)/shard_map/ain,akpn->aikp/dot_general | solution.py:56
  257.4 2.5 fusion.3
  261.1 1.0 fusion.4
  (87 shorter events, 3.2 us)
Async XLA Ops:
  6.5 1.2 copy-start
  6.5 234.8 %all-gather.3.cloned.1.call-start = ((), (), s32[]{:S(2)}) async-start(), calls=%async_computation | async-start | bytes 5242880 | tf_op jit(solution)/shard_map/all_gather | solution.py:28
  9.0 14.0 %copy-start.5 = (bf16[16,8,1024]{2,1,0:T(8,128)(2,1)}, bf16[16,8,1024]{2,1,0:T(8,128)(2,1)S(1)}, u32[]{:S(2)}) copy-start(bf16[16,8,1024]{2,1,0:T(8,128)(2,1)S(1)} %convolution_convert_fusion) | copy-start | bytes 786436
  9.0 5.7 %collective-permute-start.2 = (bf16[1,8,512]{2,1,0:T(8,128)(2,1)S(1)}, bf16[1,8,512]{2,1,0:T(8,128)(2,1)S(1)}, u32[]{:S(2)}, u32[]{:S(2)}) collective-permute-start(bf16[1,8,512]{2,1,0:T(8,128)(2,1)S(1)} %get-tuple-element.190), channel_id=1, source_target_pairs={{4,0},{8,4},{12,8},{5,1},{9,5},{13,9},{6,2},{10,6},{14,10},{7,3},{... | collective-permute-start | bytes 24584 | tf_op jit(solution)/shard_map/ppermute | solution.py:15
  11.6 3.8 %collective-permute-start.1 = (bf16[1,8,512]{2,1,0:T(8,128)(2,1)S(1)}, bf16[1,8,512]{2,1,0:T(8,128)(2,1)S(1)}, u32[]{:S(2)}, u32[]{:S(2)}) collective-permute-start(bf16[1,8,512]{2,1,0:T(8,128)(2,1)S(1)} %get-tuple-element.189), channel_id=1, source_target_pairs={{0,4},{4,8},{8,12},{1,5},{5,9},{9,13},{2,6},{6,10},{10,14},{3,7},{... | collective-permute-start | bytes 24584 | tf_op jit(solution)/shard_map/ppermute | solution.py:12
  14.7 9.6 %copy-start.21 = (bf16[512,32]{0,1:T(8,128)(2,1)S(1)}, bf16[512,32]{0,1:T(8,128)(2,1)}, u32[]{:S(2)}) copy-start(bf16[512,32]{0,1:T(8,128)(2,1)} %param.21) | copy-start | bytes 98308
  14.7 9.6 %copy-start.23 = (f32[32]{0:T(128)S(1)}, f32[32]{0:T(128)}, u32[]{:S(2)}) copy-start(f32[32]{0:T(128)} %param.22) | copy-start | bytes 388
  15.5 4.4 %collective-permute-start.4 = (bf16[18,1,512]{2,1,0:T(2,128)(2,1)S(1)}, bf16[18,1,512]{2,1,0:T(2,128)(2,1)S(1)}, u32[]{:S(2)}, u32[]{:S(2)}) collective-permute-start(bf16[18,1,512]{2,1,0:T(2,128)(2,1)S(1)} %get-tuple-element.192), channel_id=1, source_target_pairs={{1,0},{2,1},{3,2},{5,4},{6,5},{7,6},{9,8},{10,9},{11,10},{13,12},{... | collective-permute-start | bytes 55304 | tf_op jit(solution)/shard_map/ppermute | solution.py:15
  17.6 5.2 %collective-permute-start.3 = (bf16[18,1,512]{2,1,0:T(2,128)(2,1)S(1)}, bf16[18,1,512]{2,1,0:T(2,128)(2,1)S(1)}, u32[]{:S(2)}, u32[]{:S(2)}) collective-permute-start(bf16[18,1,512]{2,1,0:T(2,128)(2,1)S(1)} %get-tuple-element.191), channel_id=1, source_target_pairs={{0,1},{1,2},{2,3},{4,5},{5,6},{6,7},{8,9},{9,10},{10,11},{12,13},{... | collective-permute-start | bytes 55304 | tf_op jit(solution)/shard_map/ppermute | solution.py:12
  19.9 4.7 %copy-start.9 = (bf16[512,256]{1,0:T(8,128)(2,1)S(1)}, bf16[512,256]{1,0:T(8,128)(2,1)}, u32[]{:S(2)}) copy-start(bf16[512,256]{1,0:T(8,128)(2,1)} %param.20) | copy-start | bytes 786436
  22.9 1.8 copy-start.19
  32.8 4.3 %copy-start.2 = (bf16[16,8,16,32]{3,2,1,0:T(8,128)(2,1)S(1)}, bf16[16,8,16,32]{3,2,1,0:T(8,128)(2,1)}, u32[]{:S(2)}) copy-start(bf16[16,8,16,32]{3,2,1,0:T(8,128)(2,1)} %reshape.111) | copy-start | bytes 393220
  50.6 48.8 %collective-permute-start = (f32[16,16,2048]{2,1,0:T(8,128)}, f32[16,16,2048]{2,1,0:T(8,128)}, u32[]{:S(2)}, u32[]{:S(2)}) collective-permute-start(f32[16,16,2048]{2,1,0:T(8,128)} %get-tuple-element.293), channel_id=1, source_target_pairs={{0,1},{1,2},{2,3},{4,5},{5,6},{6,7},{8,9},{9,10},{10,11},{12,13},{... | collective-permute-start | bytes 6291464 | tf_op jit(solution)/shard_map/while/body/eval_jaxpr/ppermute | solution.py:23
  102.6 47.9 %collective-permute-start = (f32[16,16,2048]{2,1,0:T(8,128)}, f32[16,16,2048]{2,1,0:T(8,128)}, u32[]{:S(2)}, u32[]{:S(2)}) collective-permute-start(f32[16,16,2048]{2,1,0:T(8,128)} %get-tuple-element.293), channel_id=1, source_target_pairs={{0,1},{1,2},{2,3},{4,5},{5,6},{6,7},{8,9},{9,10},{10,11},{12,13},{... | collective-permute-start | bytes 6291464 | tf_op jit(solution)/shard_map/while/body/eval_jaxpr/ppermute | solution.py:23
  153.7 47.0 %collective-permute-start = (f32[16,16,2048]{2,1,0:T(8,128)}, f32[16,16,2048]{2,1,0:T(8,128)}, u32[]{:S(2)}, u32[]{:S(2)}) collective-permute-start(f32[16,16,2048]{2,1,0:T(8,128)} %get-tuple-element.293), channel_id=1, source_target_pairs={{0,1},{1,2},{2,3},{4,5},{5,6},{6,7},{8,9},{9,10},{10,11},{12,13},{... | collective-permute-start | bytes 6291464 | tf_op jit(solution)/shard_map/while/body/eval_jaxpr/ppermute | solution.py:23
  203.9 5.0 %copy-start.13 = (f32[16,8,16]{2,1,0:T(8,128)S(1)}, f32[16,8,16]{2,1,0:T(8,128)}, u32[]{:S(2)}) copy-start(f32[16,8,16]{2,1,0:T(8,128)} %get-tuple-element.204) | copy-start | bytes 24580
  203.9 5.2 %copy-start.12 = (f32[16,8,16]{2,1,0:T(8,128)S(1)}, f32[16,8,16]{2,1,0:T(8,128)}, u32[]{:S(2)}) copy-start(f32[16,8,16]{2,1,0:T(8,128)} %get-tuple-element.200) | copy-start | bytes 24580
  203.9 15.4 %copy-start.10 = (f32[8,16,64]{2,0,1:T(8,128)S(1)}, f32[8,16,64]{2,0,1:T(8,128)}, u32[]{:S(2)}) copy-start(f32[8,16,64]{2,0,1:T(8,128)} %get-tuple-element.193) | copy-start | bytes 98308
  203.9 15.4 %copy-start.11 = (f32[8,16,64]{2,0,1:T(8,128)S(1)}, f32[8,16,64]{2,0,1:T(8,128)}, u32[]{:S(2)}) copy-start(f32[8,16,64]{2,0,1:T(8,128)} %get-tuple-element.196) | copy-start | bytes 98308
  203.9 15.7 %copy-start.3 = (bf16[16,8,16,32]{3,2,1,0:T(8,128)(2,1)S(1)}, bf16[16,8,16,32]{3,2,1,0:T(8,128)(2,1)}, u32[]{:S(2)}) copy-start(bf16[16,8,16,32]{3,2,1,0:T(8,128)(2,1)} %reshape.111) | copy-start | bytes 393220
  203.9 15.7 %copy-start.17 = (f32[8,16,16]{1,2,0:T(8,128)S(1)}, f32[8,16,16]{1,2,0:T(8,128)}, u32[]{:S(2)}) copy-start(f32[8,16,16]{1,2,0:T(8,128)} %copy.61) | copy-start | bytes 24580
  203.9 15.7 %copy-start.18 = (pred[16,16]{1,0:T(8,128)(4,1)S(1)}, pred[16,16]{1,0:T(8,128)(4,1)}, u32[]{:S(2)}) copy-start(pred[16,16]{1,0:T(8,128)(4,1)} %iota_compare_fusion) | copy-start | bytes 772
  221.7 19.6 %copy-start.1 = (f32[8,16,2048]{2,1,0:T(8,128)S(1)}, f32[8,16,2048]{2,1,0:T(8,128)}, u32[]{:S(2)}) copy-start(f32[8,16,2048]{2,1,0:T(8,128)} %custom-call.1) | copy-start | bytes 3145732
  241.3 4.6 %copy-start.8 = (bf16[8,16,2048]{2,1,0:T(8,128)(2,1)S(1)}, bf16[8,16,2048]{2,1,0:T(8,128)(2,1)}, u32[]{:S(2)}) copy-start(bf16[8,16,2048]{2,1,0:T(8,128)(2,1)} %param.17) | copy-start | bytes 1572868
  249.1 8.3 %copy-start.4 = (bf16[16,8,16,32]{3,2,1,0:T(8,128)(2,1)S(1)}, bf16[16,8,16,32]{3,2,1,0:T(8,128)(2,1)}, u32[]{:S(2)}) copy-start(bf16[16,8,16,32]{3,2,1,0:T(8,128)(2,1)} %reshape.111) | copy-start | bytes 393220
  249.1 8.3 %copy-start.7 = (f32[16,8,16,32]{3,1,2,0:T(8,128)S(1)}, f32[16,8,16,32]{3,1,2,0:T(8,128)}, u32[]{:S(2)}) copy-start(f32[16,8,16,32]{3,1,2,0:T(8,128)} %convolution_multiply_fusion) | copy-start | bytes 786436
  249.1 8.3 %copy-start.14 = (f32[16,8,16]{1,2,0:T(8,128)S(1)}, f32[16,8,16]{1,2,0:T(8,128)}, u32[]{:S(2)}) copy-start(f32[16,8,16]{1,2,0:T(8,128)} %copy.53) | copy-start | bytes 24580
  249.1 8.3 %copy-start.15 = (f32[16,8,16]{1,2,0:T(8,128)S(1)}, f32[16,8,16]{1,2,0:T(8,128)}, u32[]{:S(2)}) copy-start(f32[16,8,16]{1,2,0:T(8,128)} %copy.71) | copy-start | bytes 24580
  249.1 8.3 %copy-start.16 = (f32[16,8,16]{1,2,0:T(8,128)S(1)}, f32[16,8,16]{1,2,0:T(8,128)}, u32[]{:S(2)}) copy-start(f32[16,8,16]{1,2,0:T(8,128)} %copy.55) | copy-start | bytes 24580
  249.1 8.3 %copy-start.24 = (f32[16]{0:T(128)S(1)}, f32[16]{0:T(128)}, u32[]{:S(2)}) copy-start(f32[16]{0:T(128)} %param.25) | copy-start | bytes 196
  249.1 8.3 %copy-start.25 = (pred[8,8]{1,0:T(8,128)(4,1)S(1)}, pred[8,8]{1,0:T(8,128)(4,1)}, u32[]{:S(2)}) copy-start(pred[8,8]{1,0:T(8,128)(4,1)} %iota_compare_fusion.1) | copy-start | bytes 196
  249.1 8.3 %copy-start.26 = (f32[8,16,32,16]{2,3,1,0:T(8,128)S(1)}, f32[8,16,32,16]{2,3,1,0:T(8,128)}, u32[]{:S(2)}) copy-start(f32[8,16,32,16]{2,3,1,0:T(8,128)} %fusion.11) | copy-start | bytes 786436
  259.9 1.0 copy-start.6
  259.9 1.1 copy-start.20
  259.9 1.1 copy-start.22
Sparse Core Ops, SparseCore 0:
  32.9 37.2 all-gather.2
where the time goes:
time: 270 us; the launch traced here: 269 us
  waiting for transfers between devices  144 us (53%)
  matrix products  48.9 us (18%)
  local copies, waits for them, and re-layouts  22 us (8%)
  other arithmetic  19.1 us (7%)
  between operations  13.9 us (5%)
  starting transfers between devices  12.8 us (5%)
  blocking collectives  8.39 us (3%)
    ppermute x3, waiting for transfers between devices, from_behind(): return lax.ppermute(array, axis, pairs)  140 us
    dot_general x2, matrix products, carried(): jnp.einsum('ain,akpn->aikp', c_in, entering, precision=lax.Precision.HIGH...  27.8 us
    dot_general x2, matrix products, block_sweep(): jnp.einsum('ajk,ajkp,ajn->akpn', tail, values, b_in, precision=lax.Precis...  13.4 us
    add x3, other arithmetic, advance_across(): return (entering, total_across[..., None] * entering + end_across)  9.49 us
    all_gather x1, blocking collectives, carried_in(): pieces = jax.tree.map(lambda part: lax.all_gather(part, axis), value)  8.39 us
  transfers between devices with their start and end apart: 8, of which 5 were waited for; matrix products, arithmetic and copies ran while one was open for 21% of the time, Pallas kernels for 0%

commit v1 on v0

v1 whole, which is shorter than its diff:
```python
import functools

import jax
import jax.numpy as jnp
from jax import lax
from jax.experimental import pallas as pl
from jax.experimental.pallas import tpu as pltpu
from jax.sharding import PartitionSpec as P

F32 = jnp.float32
BF16 = jnp.bfloat16
NEIGHBOURS = ((-1, 0), (1, 0), (0, -1), (0, 1), (-1, -1), (-1, 1), (1, -1), (1, 1))
OPPOSITE = (1, 0, 3, 2, 7, 6, 5, 4)
STRIP = 16
LANES = 128


def dot(a, b):
    return jnp.dot(a, b, preferred_element_type=F32)


def dot_nt(a, b):
    return lax.dot_general(a, b, (((1,), (1,)), ((), ())), preferred_element_type=F32)


def split_dot(mask, x):
    high = x.astype(BF16)
    rest = x - high.astype(F32)
    middle = rest.astype(BF16)
    low = (rest - middle.astype(F32)).astype(BF16)
    return dot(mask, high) + dot(mask, middle) + dot(mask, low)


def expand(x, spread):
    high = x.astype(BF16)
    low = (x - high.astype(F32)).astype(BF16)
    return dot(high, spread) + dot(low, spread)


def softplus(x):
    return jnp.maximum(x, 0.0) + jnp.log1p(jnp.exp(-jnp.abs(x)))


def silu(x):
    return x / (1.0 + jnp.exp(-x))


def kernel(
    nr, nc, R, C, heads,
    tok, top, win, wm, wout, small, out,
    edge, halo, halo_f, pad, gate, vals, rva, rvd, acc, weighted, y_ref,
    hs_sem, hr_sem, as_sem, ar_sem, ds_sem, dr_sem,
):
    count = R * C
    inner = wout.shape[0]
    state = (wm.shape[1] - LANES) // 4
    width = inner // heads
    i = lax.axis_index("rows")
    j = lax.axis_index("cols")
    mesh = pl.DeviceIdType.MESH

    def exists(k):
        di, dj = NEIGHBOURS[k]
        a, b = i + di, j + dj
        return (a >= 0) & (a < nr) & (b >= 0) & (b < nc)

    def target(k):
        di, dj = NEIGHBOURS[k]
        return {"rows": i + di, "cols": j + dj}

    barrier = pltpu.get_barrier_semaphore()
    for d in range(1, nc):
        pl.semaphore_signal(
            barrier, inc=1, device_id={"cols": lax.rem(j + d, nc)}, device_id_type=mesh
        )
    for d in range(1, nr):
        pl.semaphore_signal(
            barrier, inc=1, device_id={"rows": lax.rem(i + d, nr)}, device_id_type=mesh
        )
    for k in range(4, 8):
        @pl.when(exists(k))
        def _(k=k):
            pl.semaphore_signal(barrier, inc=1, device_id=target(k), device_id_type=mesh)

    pos = lax.broadcasted_iota(jnp.int32, (2 * R, count), 0)
    src = lax.broadcasted_iota(jnp.int32, (2 * R, count), 1)
    wanted = jnp.where(pos < R, pos * C, (pos - R) * C + C - 1)
    edge[...] = dot((src == wanted).astype(F32).astype(BF16), tok[...]).astype(BF16)
    corners = sum(jnp.where(exists(k), 1, 0) for k in range(4, 8))
    pl.semaphore_wait(barrier, nc - 1 + nr - 1 + corners)

    def halo_copy(k):
        di, dj = NEIGHBOURS[k]
        if di < 0:
            piece = tok.at[pl.ds(0, STRIP)]
        elif di > 0:
            piece = tok.at[pl.ds(count - STRIP, STRIP)]
        else:
            piece = edge.at[pl.ds(0 if dj < 0 else R, STRIP)]
        return pltpu.make_async_remote_copy(
            src_ref=piece,
            dst_ref=halo.at[pl.ds(OPPOSITE[k] * STRIP, STRIP)],
            send_sem=hs_sem.at[k],
            recv_sem=hr_sem.at[OPPOSITE[k]],
            device_id=target(k),
            device_id_type=mesh,
        )

    for k in range(8):
        @pl.when(exists(k))
        def _(k=k):
            halo_copy(k).start()

        @pl.when(jnp.logical_not(exists(k)))
        def _(k=k):
            halo[pl.ds(k * STRIP, STRIP)] = jnp.zeros((STRIP, halo.shape[1]), BF16)

    projected = dot(tok[...], win[...])
    gate[...] = silu(projected[:, inner:].astype(BF16).astype(F32))
    mixer = projected[:, :inner].astype(BF16).astype(F32)
    pad[pl.ds(1, R), pl.ds(8, C), :] = mixer.reshape(R, C, inner)

    for k in range(8):
        @pl.when(exists(k))
        def _(k=k):
            pltpu.make_async_remote_copy(
                src_ref=edge.at[pl.ds(0, STRIP)],
                dst_ref=halo.at[pl.ds(k * STRIP, STRIP)],
                send_sem=hs_sem.at[k],
                recv_sem=hr_sem.at[k],
                device_id=target(k),
                device_id_type=mesh,
            ).wait_recv()

    halo_f[...] = dot(halo[...], win[:, :inner]).astype(BF16).astype(F32)

    def halo_rows(k, first, n):
        return halo_f[pl.ds(k * STRIP + first, n), :]

    pad[0, pl.ds(8, C), :] = halo_rows(0, STRIP - C, C)
    pad[R + 1, pl.ds(8, C), :] = halo_rows(1, 0, C)
    for r in range(R):
        pad[1 + r, pl.ds(7, 1), :] = halo_rows(2, r, 1)
        pad[1 + r, pl.ds(8 + C, 1), :] = halo_rows(3, r, 1)
    pad[0, pl.ds(7, 1), :] = halo_rows(4, STRIP - 1, 1)
    pad[0, pl.ds(8 + C, 1), :] = halo_rows(5, STRIP - C, 1)
    pad[R + 1, pl.ds(7, 1), :] = halo_rows(6, C - 1, 1)
    pad[R + 1, pl.ds(8 + C, 1), :] = halo_rows(7, 0, 1)

    summed = jnp.zeros((R, C, inner), F32)
    for b in range(3):
        moved = pad[:, pl.ds(7 + b, C), :]
        for a in range(3):
            tap = small[pl.ds(3 * a + b, 1), :].reshape(1, 1, inner)
            summed = summed + tap * moved[a : a + R]
    values_f = silu(summed).reshape(count, inner).astype(BF16).astype(F32)
    vals[...] = values_f.astype(BF16)

    def send_a(d):
        return pltpu.make_async_remote_copy(
            src_ref=vals,
            dst_ref=rva.at[j],
            send_sem=as_sem.at[d],
            recv_sem=ar_sem.at[j],
            device_id={"cols": j + d},
            device_id_type=mesh,
        )

    def send_d(d):
        return pltpu.make_async_remote_copy(
            src_ref=vals,
            dst_ref=rvd.at[i],
            send_sem=ds_sem.at[d],
            recv_sem=dr_sem.at[i],
            device_id={"rows": i + d},
            device_id_type=mesh,
        )

    for d in range(1, max(nc, nr)):
        if d < nc:
            @pl.when(j + d < nc)
            def _(d=d):
                send_a(d).start()
        if d < nr:
            @pl.when(i + d < nr)
            def _(d=d):
                send_d(d).start()

    q = lax.broadcasted_iota(jnp.int32, (count, count), 0)
    k_ = lax.broadcasted_iota(jnp.int32, (count, count), 1)
    same_row = lax.div(q, C) == lax.div(k_, C)
    same_col = lax.rem(q, C) == lax.rem(k_, C)
    upto = k_ <= q
    after = k_ > q

    def as_mask(m):
        return jnp.where(m, 1.0, 0.0).astype(BF16)

    lane = lax.broadcasted_iota(jnp.int32, (count, LANES), 1)
    spot = lax.broadcasted_iota(jnp.int32, (LANES, inner), 0)
    head = lax.div(lax.broadcasted_iota(jnp.int32, (LANES, inner), 1), width)
    spread_a = as_mask(spot == head)
    spread_d = as_mask(spot == head + heads)
    bias = small[pl.ds(11, 1), :LANES]
    rate = small[pl.ds(12, 1), :LANES]

    maps = dot(vals[...], wm[...])
    steps = softplus(maps[:, 4 * state :] + bias)
    log_decay = -steps * rate
    cum_a = split_dot(as_mask(same_row & upto), log_decay)
    cum_d = split_dot(as_mask(same_col & upto), log_decay)
    map_a = maps[:, : 2 * state]
    map_d = maps[:, 2 * state : 4 * state]
    c_a = jnp.where(lane < state, pltpu.roll(map_a, state, 1), 0.0).astype(BF16)
    c_d = jnp.where(lane < state, pltpu.roll(map_d, state, 1), 0.0).astype(BF16)
    score_a = jnp.where(same_row & upto, dot_nt(c_a, map_a.astype(BF16)), 0.0)
    score_d = jnp.where(same_col & upto, dot_nt(c_d, map_d.astype(BF16)), 0.0)
    weighted[pl.ds(0, count), :] = (values_f * expand(steps, spread_a)).astype(BF16)
    weighted[pl.ds(count, count), :] = (values_f * expand(steps, spread_d)).astype(BF16)
    cum_at = cum_a.T
    cum_dt = cum_d.T
    per_group = LANES // width
    for g in range(inner // LANES):
        total = jnp.zeros((count, LANES), F32)
        for e in range(per_group):
            h = g * per_group + e
            diff_a = cum_a[:, h : h + 1] - cum_at[h : h + 1, :]
            hd = heads + h
            diff_d = cum_d[:, hd : hd + 1] - cum_dt[hd : hd + 1, :]
            mix_a = (jnp.exp(jnp.minimum(diff_a, 0.0)) * score_a).astype(BF16)
            mix_d = (jnp.exp(jnp.minimum(diff_d, 0.0)) * score_d).astype(BF16)
            mix = jnp.concatenate([mix_a, mix_d], axis=1)
            part = dot(mix, weighted[:, g * LANES : (g + 1) * LANES])
            total = jnp.where(lax.div(lane, width) == e, part, total)
        y_ref[:, g * LANES : (g + 1) * LANES] = total

    column = lax.rem(lax.broadcasted_iota(jnp.int32, (count, state), 0), C)
    c_top = c_d[:, :state].astype(F32)
    from_top = jnp.zeros((count, inner), F32)
    for c in range(C):
        rows = jnp.where(column == c, c_top, 0.0).astype(BF16)
        from_top = from_top + dot_nt(rows, top[pl.ds(c * inner, inner), :])

    def remote(buffer, slot, c_map, first, same, spread, gap):
        block = buffer[slot]
        m = dot(block, wm[:, first : first + 2 * state]).astype(BF16)
        s = softplus(dot(block, wm[:, 4 * state :]) + bias)
        ld = -s * rate
        tail = split_dot(as_mask(same & after), ld)
        whole = split_dot(as_mask(same), ld)
        weight = s * jnp.exp(tail + gap)
        entry = (block.astype(F32) * expand(weight, spread)).astype(BF16)
        score = jnp.where(same, dot_nt(c_map, m), 0.0).astype(BF16)
        acc[...] += dot(score, entry)
        return gap + whole

    acc[...] = jnp.zeros_like(acc)

    def hop_a(t, gap):
        slot = j - 1 - t
        pltpu.make_async_remote_copy(
            src_ref=vals, dst_ref=rva.at[slot], send_sem=as_sem.at[0],
            recv_sem=ar_sem.at[slot], device_id={"cols": slot}, device_id_type=mesh,
        ).wait_recv()
        return remote(rva, slot, c_a, 0, same_row, spread_a, gap)

    lax.fori_loop(0, j, hop_a, jnp.zeros((count, LANES), F32))
    y_ref[...] += expand(jnp.exp(cum_a), spread_a) * acc[...]
    acc[...] = jnp.zeros_like(acc)

    def hop_d(t, gap):
        slot = i - 1 - t
        pltpu.make_async_remote_copy(
            src_ref=vals, dst_ref=rvd.at[slot], send_sem=ds_sem.at[0],
            recv_sem=dr_sem.at[slot], device_id={"rows": slot}, device_id_type=mesh,
        ).wait_recv()
        return remote(rvd, slot, c_d, 2 * state, same_col, spread_d, gap)

    gap_d = lax.fori_loop(0, i, hop_d, jnp.zeros((count, LANES), F32))
    y = (
        y_ref[...]
        + expand(jnp.exp(cum_d), spread_d) * acc[...]
        + expand(jnp.exp(cum_d + gap_d), spread_d) * from_top
        + small[pl.ds(10, 1), :] * vals[...].astype(F32)
    )
    gated = y * gate[...]
    scale = lax.rsqrt(jnp.mean(gated * gated, axis=-1, keepdims=True) + 1e-05)
    normed = (gated * scale * small[pl.ds(9, 1), :]).astype(BF16)
    out[...] = dot(normed, wout[...]).astype(BF16)

    for k in range(8):
        @pl.when(exists(k))
        def _(k=k):
            halo_copy(k).wait_send()
    for d in range(1, nc):
        @pl.when(j + d < nc)
        def _(d=d):
            send_a(d).wait_send()
    for d in range(1, nr):
        @pl.when(i + d < nr)
        def _(d=d):
            send_d(d).wait_send()


def shards(
    nr, nc,
    tokens, top_state, in_weight, conv_weight, bc_weight, step_weight, step_bias,
    across_rate, down_rate, skip_gain, norm_gain, out_weight,
):
    R, C, model = tokens.shape
    inner = out_weight.shape[0]
    heads = across_rate.shape[0]
    state = bc_weight.shape[1] // 4
    count = R * C
    wm = jnp.pad(
        jnp.concatenate([bc_weight, step_weight], axis=1), ((0, 0), (0, LANES - 2 * heads))
    )

    def row(x):
        return jnp.pad(x, (0, inner - x.shape[0]))[None]

    small = jnp.concatenate(
        [
            conv_weight,
            norm_gain[None],
            jnp.repeat(skip_gain, inner // heads)[None],
            row(step_bias),
            row(jnp.concatenate([across_rate, down_rate])),
            jnp.zeros((3, inner), F32),
        ],
        axis=0,
    )
    vmem = pl.BlockSpec(memory_space=pltpu.VMEM)
    result = pl.pallas_call(
        functools.partial(kernel, nr, nc, R, C, heads),
        out_shape=jax.ShapeDtypeStruct((count, model), BF16),
        in_specs=[vmem] * 6,
        out_specs=vmem,
        scratch_shapes=[
            pltpu.VMEM((2 * R, model), BF16),
            pltpu.VMEM((8 * STRIP, model), BF16),
            pltpu.VMEM((8 * STRIP, inner), F32),
            pltpu.VMEM((R + 2, 24, inner), F32),
            pltpu.VMEM((count, inner), F32),
            pltpu.VMEM((count, inner), BF16),
            pltpu.VMEM((nc, count, inner), BF16),
            pltpu.VMEM((nr, count, inner), BF16),
            pltpu.VMEM((count, inner), F32),
            pltpu.VMEM((2 * count, inner), BF16),
            pltpu.VMEM((count, inner), F32),
            pltpu.SemaphoreType.DMA((8,)),
            pltpu.SemaphoreType.DMA((8,)),
            pltpu.SemaphoreType.DMA((nc,)),
            pltpu.SemaphoreType.DMA((nc,)),
            pltpu.SemaphoreType.DMA((nr,)),
            pltpu.SemaphoreType.DMA((nr,)),
        ],
        compiler_params=pltpu.CompilerParams(
            collective_id=0, has_side_effects=True, vmem_limit_bytes=40 * 1024 * 1024
        ),
    )(
        tokens.reshape(count, model),
        top_state.reshape(C * inner, state),
        in_weight,
        wm,
        out_weight,
        small,
    )
    return result.reshape(R, C, model)


def solution(mesh):
    in_specs = (
        P(("groups", "rows"), "cols", None),
        P(("groups", "cols"), None, None),
    ) + (P(),) * 10
    out_specs = P(("groups", "rows"), "cols", None)
    return jax.shard_map(
        functools.partial(shards, mesh.shape["rows"], mesh.shape["cols"]),
        mesh=mesh, in_specs=in_specs, out_specs=out_specs, check_vma=False,
    )
```

time: 270 us -> 32.2 us (0.12)
  the two profiles are of different devices: /device:TPU:25 before, /device:TPU:29 now
where the time goes in v1:
time: 32.2 us; the launch traced here: 31.8 us
  Pallas kernels  24.3 us (75%)
  local copies, waits for them, and re-layouts  6.71 us (21%)
  other arithmetic  0.79 us (2%)
    pallas_call x1, Pallas kernels, shards(): pl.pallas_call(functools.partial(kernel, nr, nc, R, C, heads), out_shape=...  24.3 us
    reshape x1, local copies, waits for them, and re-layouts, shards(): top_state.reshape(C * inner, state)  2.18 us
    unnamed x10, local copies, waits for them, and re-layouts  1.56 us
    concatenate x1, local copies, waits for them, and re-layouts, shards(): jnp.concatenate([conv_weight, norm_gain[None], jnp.repeat(skip_gain, inne...  1.47 us
    concatenate x1, other arithmetic, shards(): jnp.concatenate([across_rate, down_rate])  0.75 us
    broadcast_in_dim x1, local copies, waits for them, and re-layouts, shards(): jnp.repeat(skip_gain, inner // heads)[None]  0.72 us
    pad x1, local copies, waits for them, and re-layouts, row(): return jnp.pad(x, (0, inner - x.shape[0]))[None]  0.7 us

profile of v1, /device:TPU:29, one launch (start us, length us, event | category | flops | bytes accessed | tf_op | source)
XLA Modules:
  0.0 31.8 jit_solution(17273909008366401510)
XLA Ops:
  0.0 0.0 copy-start.3
  0.0 0.7 %pad.12 = f32[512]{0:T(512)S(1)} pad(f32[32]{0:T(128)} %param.18, f32[]{:T(128)} %constant.5.clone.1), padding=0_480 | pad | bytes 2180 | tf_op jit(solution)/shard_map/jit(_pad)/pad | solution.py:320
  0.7 0.7 %select_maximum_fusion = f32[512]{0:T(512)S(1)} fusion(f32[16]{0:T(128)} %param.20, f32[16]{0:T(128)} %param.19), kind=kLoop, calls=%fused_computation.4 | loop fusion | flops 2048 | bytes 2176 | tf_op jit(solution)/shard_map/concatenate | solution.py:328
  1.5 0.7 %broadcast_in_dim.16 = f32[16,32]{1,0:T(8,128)S(1)} broadcast(f32[16]{0:T(128)} %param.21), dimensions={0} | broadcast | bytes 2112 | tf_op jit(solution)/shard_map/broadcast_in_dim | solution.py:326
  2.2 0.1 broadcast_in_dim_reshape.3
  2.3 1.5 %concatenate.11.small = f32[16,512]{1,0:T(8,128)S(1)} concatenate(f32[9,512]{1,0:T(8,128)} %param.15, f32[1,512]{1,0:T(1,128)} %bitcast.9, f32[1,512]{1,0:T(1,128)S(1)} %broadcast_in_dim_reshape.3, f32[1,512]{1,0:T(1,128)S(1)} %bitcast.7, f32[1,512]{1,0:T(1,128)S(1)} %bitcast.8, f32[3,512]{1,0:T(4,128)S(1)} %broadcast_in_dim.19), dimensions={0} | concatenate | bytes 65536 | tf_op jit(solution)/shard_map/concatenate | solution.py:322
  3.7 0.9 %copy.14 = bf16[512,32]{1,0:T(8,128)(2,1)S(1)} copy(bf16[512,32]{0,1:T(8,128)(2,1)} %param.17) | data formatting | bytes 65536 | tf_op args[5]
  4.6 0.0 copy-done.3
  4.6 0.0 copy-start
  4.7 0.0 copy-start.1
  4.7 0.0 copy-start.2
  4.7 2.2 %reshape.10.top = bf16[4096,64]{1,0:T(8,128)(2,1)S(1)} reshape(bf16[8,16,2048]{2,1,0:T(8,128)(2,1)} %param.13) | data formatting | bytes 1048576 | tf_op jit(solution)/shard_map/reshape | solution.py:363
  6.9 0.0 copy-done
  6.9 0.0 copy-done.1
  6.9 0.0 copy-done.2
  6.9 24.3 %shard_map.118 = bf16[128,512]{1,0:T(8,128)(2,1)S(1)} custom-call(bf16[128,512]{1,0:T(8,128)(2,1)S(1)} %bitcast.6, bf16[4096,64]{1,0:T(8,128)(2,1)S(1)} %reshape.10.top, bf16[512,1024]{1,0:T(8,128)(2,1)S(1)} %copy-done, bf16[512,384]{1,0:T(8,128)(2,1)S(1)} %fusion.2.wm, bf16[512,512]{1,0:T(8,128)(2,1)S(1)} %copy-done.1, f32[16,512]{1,0:T(8,128)S(1)} %concatenate.11.small), custom_call_target="tpu_custom_call" | custom-call | tf_op jit(solution)/shard_map/pallas_call | solution.py:334
  31.2 0.7 %copy.16 = bf16[16,8,512]{2,1,0:T(8,128)(2,1)} copy(bf16[16,8,512]{2,1,0:T(8,128)(2,1)S(1)} %bitcast.5) | data formatting | bytes 262144
  (2 shorter events, 0.0 us)
Async XLA Ops:
  0.0 4.6 %copy-start.3 = (bf16[512,256]{1,0:T(8,128)(2,1)S(1)}, bf16[512,256]{1,0:T(8,128)(2,1)}, u32[]{:S(2)}) copy-start(bf16[512,256]{1,0:T(8,128)(2,1)} %param.16) | copy-start | bytes 786436
  4.6 2.3 %copy-start = (bf16[512,1024]{1,0:T(8,128)(2,1)S(1)}, bf16[512,1024]{1,0:T(8,128)(2,1)}, u32[]{:S(2)}) copy-start(bf16[512,1024]{1,0:T(8,128)(2,1)} %win.1) | copy-start | bytes 3145732
  4.7 2.2 %copy-start.1 = (bf16[512,512]{1,0:T(8,128)(2,1)S(1)}, bf16[512,512]{1,0:T(8,128)(2,1)}, u32[]{:S(2)}) copy-start(bf16[512,512]{1,0:T(8,128)(2,1)} %wout.1) | copy-start | bytes 1572868
  4.7 2.2 %copy-start.2 = (bf16[16,8,512]{2,1,0:T(8,128)(2,1)S(1)}, bf16[16,8,512]{2,1,0:T(8,128)(2,1)}, u32[]{:S(2)}) copy-start(bf16[16,8,512]{2,1,0:T(8,128)(2,1)} %param.12) | copy-start | bytes 393220

commit v2 on v1

--- a/solution.py
+++ b/solution.py
@@ -31,6 +31,14 @@
     return dot(mask, high) + dot(mask, middle) + dot(mask, low)
 
 
+def split_sum(x, mask):
+    high = x.astype(BF16)
+    rest = x - high.astype(F32)
+    middle = rest.astype(BF16)
+    low = (rest - middle.astype(F32)).astype(BF16)
+    return dot(high, mask) + dot(middle, mask) + dot(low, mask)
+
+
 def expand(x, spread):
     high = x.astype(BF16)
     low = (x - high.astype(F32)).astype(BF16)
@@ -47,13 +55,13 @@
 
 def kernel(
     nr, nc, R, C, heads,
-    tok, top, win, wm, wout, small, out,
-    edge, halo, halo_f, pad, gate, vals, rva, rvd, acc, weighted, y_ref,
-    hs_sem, hr_sem, as_sem, ar_sem, ds_sem, dr_sem,
+    tok_h, top_h, win_h, wbc_h, wout_h, conv, wst_t, step_bias, rate_a, rate_d, skip, gain, out,
+    tok, top, win, wbc, wout, wst, param, edge, halo, halo_f, pad, gate, vals, rva, rvd, acc, weighted, y_ref,
+    ld_sem, hs_sem, hr_sem, as_sem, ar_sem, ds_sem, dr_sem,
 ):
     count = R * C
     inner = wout.shape[0]
-    state = (wm.shape[1] - LANES) // 4
+    state = wbc.shape[1] // 4
     width = inner // heads
     i = lax.axis_index("rows")
     j = lax.axis_index("cols")
@@ -68,6 +76,15 @@
         di, dj = NEIGHBOURS[k]
         return {"rows": i + di, "cols": j + dj}
 
+    loads = [
+        pltpu.make_async_copy(a, b, ld_sem.at[n])
+        for n, (a, b) in enumerate(
+            ((tok_h, tok), (win_h, win), (wbc_h, wbc), (top_h, top), (wout_h, wout))
+        )
+    ]
+    for load in loads:
+        load.start()
+
     barrier = pltpu.get_barrier_semaphore()
     for d in range(1, nc):
         pl.semaphore_signal(
@@ -85,6 +102,14 @@
     pos = lax.broadcasted_iota(jnp.int32, (2 * R, count), 0)
     src = lax.broadcasted_iota(jnp.int32, (2 * R, count), 1)
     wanted = jnp.where(pos < R, pos * C, (pos - R) * C + C - 1)
+    wst[...] = jnp.zeros_like(wst)
+    wst[pl.ds(0, 2 * heads), :] = wst_t[...]
+    param[...] = jnp.zeros_like(param)
+    param[0:1, 0 : 2 * heads] = step_bias[...]
+    param[1:2, 0:heads] = rate_a[...]
+    param[1:2, heads : 2 * heads] = rate_d[...]
+    param[2:3, 0:heads] = skip[...]
+    loads[0].wait()
     edge[...] = dot((src == wanted).astype(F32).astype(BF16), tok[...]).astype(BF16)
     corners = sum(jnp.where(exists(k), 1, 0) for k in range(4, 8))
     pl.semaphore_wait(barrier, nc - 1 + nr - 1 + corners)
@@ -115,6 +140,7 @@
         def _(k=k):
             halo[pl.ds(k * STRIP, STRIP)] = jnp.zeros((STRIP, halo.shape[1]), BF16)
 
+    loads[1].wait()
     projected = dot(tok[...], win[...])
     gate[...] = silu(projected[:, inner:].astype(BF16).astype(F32))
     mixer = projected[:, :inner].astype(BF16).astype(F32)
@@ -151,7 +177,7 @@
     for b in range(3):
         moved = pad[:, pl.ds(7 + b, C), :]
         for a in range(3):
-            tap = small[pl.ds(3 * a + b, 1), :].reshape(1, 1, inner)
+            tap = conv[pl.ds(3 * a + b, 1), :].reshape(1, 1, inner)
             summed = summed + tap * moved[a : a + R]
     values_f = silu(summed).reshape(count, inner).astype(BF16).astype(F32)
     vals[...] = values_f.astype(BF16)
@@ -201,11 +227,12 @@
     head = lax.div(lax.broadcasted_iota(jnp.int32, (LANES, inner), 1), width)
     spread_a = as_mask(spot == head)
     spread_d = as_mask(spot == head + heads)
-    bias = small[pl.ds(11, 1), :LANES]
-    rate = small[pl.ds(12, 1), :LANES]
-
-    maps = dot(vals[...], wm[...])
-    steps = softplus(maps[:, 4 * state :] + bias)
+    bias = param[0:1, :]
+    rate = param[1:2, :]
+
+    loads[2].wait()
+    maps = dot(vals[...], wbc[...])
+    steps = softplus(dot_nt(vals[...], wst[...]) + bias)
     log_decay = -steps * rate
     cum_a = split_dot(as_mask(same_row & upto), log_decay)
     cum_d = split_dot(as_mask(same_col & upto), log_decay)
@@ -234,17 +261,32 @@
             total = jnp.where(lax.div(lane, width) == e, part, total)
         y_ref[:, g * LANES : (g + 1) * LANES] = total
 
-    column = lax.rem(lax.broadcasted_iota(jnp.int32, (count, state), 0), C)
-    c_top = c_d[:, :state].astype(F32)
-    from_top = jnp.zeros((count, inner), F32)
-    for c in range(C):
-        rows = jnp.where(column == c, c_top, 0.0).astype(BF16)
-        from_top = from_top + dot_nt(rows, top[pl.ds(c * inner, inner), :])
+    loads[3].wait()
+    column = lax.rem(q, C)
+    c_high = pltpu.roll(c_d.astype(F32), state, 1)
+    pairs = width * state // LANES
+    halves = []
+    for c_half in (c_d.astype(F32), c_high):
+        half = jnp.zeros((count, pairs * heads), F32)
+        for c in range(C):
+            rows = jnp.where(column == c, c_half, 0.0).astype(BF16)
+            block = jnp.concatenate(
+                [top[c, :, n * LANES : (n + 1) * LANES] for n in range(pairs)], axis=0
+            )
+            half = half + dot_nt(rows, block)
+        halves.append(half)
+    lane_from = lax.broadcasted_iota(jnp.int32, (inner, inner), 0)
+    lane_to = lax.broadcasted_iota(jnp.int32, (inner, inner), 1)
+    half_size = pairs * heads
+    parity = lax.div(lane_from, half_size)
+    pair = lax.div(lax.rem(lane_from, half_size), heads)
+    moves = as_mask(lax.rem(lane_from, heads) * width + 2 * pair + parity == lane_to)
+    from_top = expand(jnp.concatenate(halves, axis=1), moves)
 
     def remote(buffer, slot, c_map, first, same, spread, gap):
         block = buffer[slot]
-        m = dot(block, wm[:, first : first + 2 * state]).astype(BF16)
-        s = softplus(dot(block, wm[:, 4 * state :]) + bias)
+        m = dot(block, wbc[:, first : first + 2 * state]).astype(BF16)
+        s = softplus(dot_nt(block, wst[...]) + bias)
         ld = -s * rate
         tail = split_dot(as_mask(same & after), ld)
         whole = split_dot(as_mask(same), ld)
@@ -281,11 +323,12 @@
         y_ref[...]
         + expand(jnp.exp(cum_d), spread_d) * acc[...]
         + expand(jnp.exp(cum_d + gap_d), spread_d) * from_top
-        + small[pl.ds(10, 1), :] * vals[...].astype(F32)
+        + split_sum(param[0:8, :], spread_a)[2:3, :] * vals[...].astype(F32)
     )
     gated = y * gate[...]
     scale = lax.rsqrt(jnp.mean(gated * gated, axis=-1, keepdims=True) + 1e-05)
-    normed = (gated * scale * small[pl.ds(9, 1), :]).astype(BF16)
+    normed = (gated * scale * gain[...]).astype(BF16)
+    loads[4].wait()
     out[...] = dot(normed, wout[...]).astype(BF16)
 
     for k in range(8):
@@ -310,33 +353,21 @@
     R, C, model = tokens.shape
     inner = out_weight.shape[0]
     heads = across_rate.shape[0]
-    state = bc_weight.shape[1] // 4
     count = R * C
-    wm = jnp.pad(
-        jnp.concatenate([bc_weight, step_weight], axis=1), ((0, 0), (0, LANES - 2 * heads))
-    )
-
-    def row(x):
-        return jnp.pad(x, (0, inner - x.shape[0]))[None]
-
-    small = jnp.concatenate(
-        [
-            conv_weight,
-            norm_gain[None],
-            jnp.repeat(skip_gain, inner // heads)[None],
-            row(step_bias),
-            row(jnp.concatenate([across_rate, down_rate])),
-            jnp.zeros((3, inner), F32),
-        ],
-        axis=0,
-    )
     vmem = pl.BlockSpec(memory_space=pltpu.VMEM)
     result = pl.pallas_call(
         functools.partial(kernel, nr, nc, R, C, heads),
         out_shape=jax.ShapeDtypeStruct((count, model), BF16),
-        in_specs=[vmem] * 6,
+        in_specs=[pl.BlockSpec(memory_space=pltpu.HBM)] * 5 + [vmem] * 7,
         out_specs=vmem,
         scratch_shapes=[
+            pltpu.VMEM((count, model), BF16),
+            pltpu.VMEM(top_state.shape, BF16),
+            pltpu.VMEM(in_weight.shape, BF16),
+            pltpu.VMEM(bc_weight.shape, BF16),
+            pltpu.VMEM(out_weight.shape, BF16),
+            pltpu.VMEM((LANES, inner), BF16),
+            pltpu.VMEM((8, LANES), F32),
             pltpu.VMEM((2 * R, model), BF16),
             pltpu.VMEM((8 * STRIP, model), BF16),
             pltpu.VMEM((8 * STRIP, inner), F32),
@@ -348,6 +379,7 @@
             pltpu.VMEM((count, inner), F32),
             pltpu.VMEM((2 * count, inner), BF16),
             pltpu.VMEM((count, inner), F32),
+            pltpu.SemaphoreType.DMA((5,)),
             pltpu.SemaphoreType.DMA((8,)),
             pltpu.SemaphoreType.DMA((8,)),
             pltpu.SemaphoreType.DMA((nc,)),
@@ -356,15 +388,21 @@
             pltpu.SemaphoreType.DMA((nr,)),
         ],
         compiler_params=pltpu.CompilerParams(
-            collective_id=0, has_side_effects=True, vmem_limit_bytes=40 * 1024 * 1024
+            collective_id=0, has_side_effects=True, vmem_limit_bytes=63 * 1024 * 1024
         ),
     )(
         tokens.reshape(count, model),
-        top_state.reshape(C * inner, state),
+        top_state,
         in_weight,
-        wm,
+        bc_weight,
         out_weight,
-        small,
+        conv_weight,
+        step_weight.T,
+        step_bias[None],
+        across_rate[None],
+        down_rate[None],
+        skip_gain[None],
+        norm_gain[None],
     )
     return result.reshape(R, C, model)
 

time: 32.2 us -> 27.9 us (0.87)
  the two profiles are of different devices: /device:TPU:29 before, /device:TPU:31 now
where the time goes in v2:
time: 27.9 us; the launch traced here: 27.7 us
  Pallas kernels  26.1 us (94%)
  local copies, waits for them, and re-layouts  1.57 us (6%)
    pallas_call x1, Pallas kernels, shards(): pl.pallas_call(functools.partial(kernel, nr, nc, R, C, heads), out_shape=...  26.1 us
    unnamed x1, local copies, waits for them, and re-layouts  1.57 us

profile of v2, /device:TPU:31, one launch (start us, length us, event | category | flops | bytes accessed | tf_op | source)
XLA Modules:
  0.0 27.7 jit_solution(10284652780353996494)
XLA Ops:
  0.0 26.1 %shard_map.118 = bf16[128,512]{1,0:T(8,128)(2,1)} custom-call(bf16[128,512]{1,0:T(8,128)(2,1)} %bitcast.9, bf16[8,16,2048]{2,1,0:T(8,128)(2,1)} %top_h.1, bf16[512,1024]{1,0:T(8,128)(2,1)} %win_h.1, bf16[512,256]{1,0:T(8,128)(2,1)} %wbc_h.1, bf16[512,512]{1,0:T(8,128)(2,1)} %wout_h.1, f32[9,512]{1,0:T(8,128)} %conv.1, bf16[32,512]{1,0:T(8,128)(2,1)} %bitcast.10, ...), custom_call_target="tpu_custom_call" | custom-call | tf_op jit(solution)/shard_map/pallas_call | solution.py:358
  26.1 1.6 %copy.14 = bf16[16,8,512]{2,1,0:T(8,128)(2,1)} copy(bf16[16,8,512]{2,1,0:T(8,128)(2,1)} %bitcast.8) | data formatting | bytes 262144

commit v3 on v2

--- a/solution.py
+++ b/solution.py
@@ -192,6 +192,24 @@
             device_id_type=mesh,
         )
 
+    relay = nc >= 4
+
+    def sends_a(d):
+        direct = j + d < nc
+        return direct & (j != nc - 3) if relay and d == 2 else direct
+
+    def arrival_a(slot):
+        return pltpu.make_async_remote_copy(
+            src_ref=vals, dst_ref=rva.at[slot], send_sem=as_sem.at[0],
+            recv_sem=ar_sem.at[slot], device_id={"cols": slot}, device_id_type=mesh,
+        )
+
+    def relayed():
+        return pltpu.make_async_remote_copy(
+            src_ref=rva.at[nc - 3], dst_ref=rva.at[nc - 3], send_sem=as_sem.at[0],
+            recv_sem=ar_sem.at[nc - 3], device_id={"cols": j + 1}, device_id_type=mesh,
+        )
+
     def send_d(d):
         return pltpu.make_async_remote_copy(
             src_ref=vals,
@@ -204,7 +222,7 @@
 
     for d in range(1, max(nc, nr)):
         if d < nc:
-            @pl.when(j + d < nc)
+            @pl.when(sends_a(d))
             def _(d=d):
                 send_a(d).start()
         if d < nr:
@@ -261,6 +279,12 @@
             total = jnp.where(lax.div(lane, width) == e, part, total)
         y_ref[:, g * LANES : (g + 1) * LANES] = total
 
+    if relay:
+        @pl.when(j == nc - 2)
+        def _():
+            arrival_a(nc - 3).wait_recv()
+            relayed().start()
+
     loads[3].wait()
     column = lax.rem(q, C)
     c_high = pltpu.roll(c_d.astype(F32), state, 1)
@@ -298,18 +322,6 @@
 
     acc[...] = jnp.zeros_like(acc)
 
-    def hop_a(t, gap):
-        slot = j - 1 - t
-        pltpu.make_async_remote_copy(
-            src_ref=vals, dst_ref=rva.at[slot], send_sem=as_sem.at[0],
-            recv_sem=ar_sem.at[slot], device_id={"cols": slot}, device_id_type=mesh,
-        ).wait_recv()
-        return remote(rva, slot, c_a, 0, same_row, spread_a, gap)
-
-    lax.fori_loop(0, j, hop_a, jnp.zeros((count, LANES), F32))
-    y_ref[...] += expand(jnp.exp(cum_a), spread_a) * acc[...]
-    acc[...] = jnp.zeros_like(acc)
-
     def hop_d(t, gap):
         slot = i - 1 - t
         pltpu.make_async_remote_copy(
@@ -319,24 +331,41 @@
         return remote(rvd, slot, c_d, 2 * state, same_col, spread_d, gap)
 
     gap_d = lax.fori_loop(0, i, hop_d, jnp.zeros((count, LANES), F32))
-    y = (
-        y_ref[...]
-        + expand(jnp.exp(cum_d), spread_d) * acc[...]
+    y_ref[...] += (
+        expand(jnp.exp(cum_d), spread_d) * acc[...]
         + expand(jnp.exp(cum_d + gap_d), spread_d) * from_top
         + split_sum(param[0:8, :], spread_a)[2:3, :] * vals[...].astype(F32)
     )
+    acc[...] = jnp.zeros_like(acc)
+
+    def hop_a(t, gap):
+        slot = j - 1 - t
+        waits = (j != nc - 2) | (slot != nc - 3) if relay else slot >= 0
+
+        @pl.when(waits)
+        def _():
+            arrival_a(slot).wait_recv()
+
+        return remote(rva, slot, c_a, 0, same_row, spread_a, gap)
+
+    lax.fori_loop(0, j, hop_a, jnp.zeros((count, LANES), F32))
+    y = y_ref[...] + expand(jnp.exp(cum_a), spread_a) * acc[...]
     gated = y * gate[...]
     scale = lax.rsqrt(jnp.mean(gated * gated, axis=-1, keepdims=True) + 1e-05)
     normed = (gated * scale * gain[...]).astype(BF16)
     loads[4].wait()
     out[...] = dot(normed, wout[...]).astype(BF16)
 
+    if relay:
+        @pl.when(j == nc - 2)
+        def _():
+            relayed().wait_send()
     for k in range(8):
         @pl.when(exists(k))
         def _(k=k):
             halo_copy(k).wait_send()
     for d in range(1, nc):
-        @pl.when(j + d < nc)
+        @pl.when(sends_a(d))
         def _(d=d):
             send_a(d).wait_send()
     for d in range(1, nr):

time: 27.9 us -> 24.9 us (0.89)
  the two profiles are of different devices: /device:TPU:31 before, /device:TPU:25 now
where the time goes in v3:
time: 24.9 us; the launch traced here: 24.7 us
  Pallas kernels  23.1 us (93%)
  local copies, waits for them, and re-layouts  1.57 us (6%)
    pallas_call x1, Pallas kernels, shards(): pl.pallas_call(functools.partial(kernel, nr, nc, R, C, heads), out_shape=...  23.1 us
    unnamed x1, local copies, waits for them, and re-layouts  1.57 us

profile of v3, /device:TPU:25, one launch (start us, length us, event | category | flops | bytes accessed | tf_op | source)
XLA Modules:
  0.0 24.7 jit_solution(131269604599995693)
XLA Ops:
  0.0 23.1 %shard_map.118 = bf16[128,512]{1,0:T(8,128)(2,1)} custom-call(bf16[128,512]{1,0:T(8,128)(2,1)} %bitcast.9, bf16[8,16,2048]{2,1,0:T(8,128)(2,1)} %top_h.1, bf16[512,1024]{1,0:T(8,128)(2,1)} %win_h.1, bf16[512,256]{1,0:T(8,128)(2,1)} %wbc_h.1, bf16[512,512]{1,0:T(8,128)(2,1)} %wout_h.1, f32[9,512]{1,0:T(8,128)} %conv.1, bf16[32,512]{1,0:T(8,128)(2,1)} %bitcast.10, ...), custom_call_target="tpu_custom_call" | custom-call | tf_op jit(solution)/shard_map/pallas_call | solution.py:387
  23.1 1.6 %copy.14 = bf16[16,8,512]{2,1,0:T(8,128)(2,1)} copy(bf16[16,8,512]{2,1,0:T(8,128)(2,1)} %bitcast.8) | data formatting | bytes 262144

commit v4 on v3

--- a/solution.py
+++ b/solution.py
@@ -222,10 +222,11 @@
 
     for d in range(1, max(nc, nr)):
         if d < nc:
-            @pl.when(sends_a(d))
-            def _(d=d):
-                send_a(d).start()
-        if d < nr:
+            if d == 1:
+                @pl.when(sends_a(d))
+                def _(d=d):
+                    send_a(d).start()
+        if d == 1:
             @pl.when(i + d < nr)
             def _(d=d):
                 send_d(d).start()
@@ -278,6 +279,16 @@
             part = dot(mix, weighted[:, g * LANES : (g + 1) * LANES])
             total = jnp.where(lax.div(lane, width) == e, part, total)
         y_ref[:, g * LANES : (g + 1) * LANES] = total
+
+    for d in range(nc - 1, 1, -1):
+        @pl.when(sends_a(d))
+        def _(d=d):
+            send_a(d).start()
+
+    for d in range(nr - 1, 1, -1):
+        @pl.when(i + d < nr)
+        def _(d=d):
+            send_d(d).start()
 
     if relay:
         @pl.when(j == nc - 2)
@@ -417,7 +428,7 @@
             pltpu.SemaphoreType.DMA((nr,)),
         ],
         compiler_params=pltpu.CompilerParams(
-            collective_id=0, has_side_effects=True, vmem_limit_bytes=63 * 1024 * 1024
+            collective_id=0, has_side_effects=True, vmem_limit_bytes=55000 * 1024
         ),
     )(
         tokens.reshape(count, model),

time: 24.9 us -> 23.1 us (0.928)
  Pallas kernels: 23.1 us -> 19.9 us
  local copies, waits for them, and re-layouts: 1.57 us -> 2.87 us
    pallas_call x1, Pallas kernels: 23.1 us -> 19.9 us  [shards(): pl.pallas_call(functools.partial(kernel, nr, nc, R, C, heads), out_shape=...]
    unnamed x1 -> x15, local copies, waits for them, and re-layouts: 1.57 us -> 2.87 us
where the time goes in v4:
time: 23.1 us; the launch traced here: 22.8 us
  Pallas kernels  19.9 us (86%)
  local copies, waits for them, and re-layouts  2.87 us (12%)
    pallas_call x1, Pallas kernels, shards(): pl.pallas_call(functools.partial(kernel, nr, nc, R, C, heads), out_shape=...  19.9 us
    unnamed x15, local copies, waits for them, and re-layouts  2.87 us

profile of v4, /device:TPU:25, one launch (start us, length us, event | category | flops | bytes accessed | tf_op | source)
XLA Modules:
  0.0 22.8 jit_solution(3607869918492637016)
XLA Ops:
  0.0 0.0 copy-start.6
  0.0 0.0 copy-start.2
  0.0 0.0 copy-start.3
  0.0 0.0 copy-start.4
  0.0 0.0 copy-start.5
  0.0 0.6 %copy-done.6 = f32[16]{0:T(128)S(1)} copy-done((f32[16]{0:T(128)S(1)}, f32[16]{0:T(128)}, u32[]{:S(2)}) %copy-start.6) | copy-done | bytes 88
  0.7 0.0 copy-done.2
  0.7 0.0 copy-done.3
  0.7 0.0 copy-done.4
  0.7 0.0 copy-done.5
  0.7 0.0 copy-start
  0.7 0.8 %copy-done = f32[9,512]{1,0:T(8,128)S(1)} copy-done((f32[9,512]{1,0:T(8,128)S(1)}, f32[9,512]{1,0:T(8,128)}, u32[]{:S(2)}) %copy-start) | copy-done | bytes 18456
  1.5 0.0 copy-start.1
  1.5 0.8 %copy-done.1 = bf16[512,32]{0,1:T(8,128)(2,1)S(1)} copy-done((bf16[512,32]{0,1:T(8,128)(2,1)S(1)}, bf16[512,32]{0,1:T(8,128)(2,1)}, u32[]{:S(2)}) %copy-start.1) | copy-done | bytes 32792
  2.2 19.9 %shard_map.118 = bf16[128,512]{1,0:T(8,128)(2,1)S(1)} custom-call(bf16[128,512]{1,0:T(8,128)(2,1)} %bitcast.15, bf16[8,16,2048]{2,1,0:T(8,128)(2,1)} %top_h.1, bf16[512,1024]{1,0:T(8,128)(2,1)} %win_h.1, bf16[512,256]{1,0:T(8,128)(2,1)} %wbc_h.1, bf16[512,512]{1,0:T(8,128)(2,1)} %wout_h.1, f32[9,512]{1,0:T(8,128)S(1)} %copy-done, ...), custom_call_target="tpu_custom_call" | custom-call | tf_op jit(solution)/shard_map/pallas_call | solution.py:398
  22.2 0.7 %copy.14 = bf16[16,8,512]{2,1,0:T(8,128)(2,1)} copy(bf16[16,8,512]{2,1,0:T(8,128)(2,1)S(1)} %bitcast.8) | data formatting | bytes 262144
Async XLA Ops:
  0.0 0.7 %copy-start.6 = (f32[16]{0:T(128)S(1)}, f32[16]{0:T(128)}, u32[]{:S(2)}) copy-start(f32[16]{0:T(128)} %param.21) | copy-start | bytes 196
  0.0 0.7 %copy-start.2 = (f32[512]{0:T(512)S(1)}, f32[512]{0:T(512)}, u32[]{:S(2)}) copy-start(f32[512]{0:T(512)} %param.22) | copy-start | bytes 6148
  0.0 0.7 %copy-start.3 = (f32[32]{0:T(128)S(1)}, f32[32]{0:T(128)}, u32[]{:S(2)}) copy-start(f32[32]{0:T(128)} %param.18) | copy-start | bytes 388
  0.0 0.7 %copy-start.4 = (f32[16]{0:T(128)S(1)}, f32[16]{0:T(128)}, u32[]{:S(2)}) copy-start(f32[16]{0:T(128)} %param.19) | copy-start | bytes 196
  0.0 0.7 %copy-start.5 = (f32[16]{0:T(128)S(1)}, f32[16]{0:T(128)}, u32[]{:S(2)}) copy-start(f32[16]{0:T(128)} %param.20) | copy-start | bytes 196
  0.7 0.8 %copy-start = (f32[9,512]{1,0:T(8,128)S(1)}, f32[9,512]{1,0:T(8,128)}, u32[]{:S(2)}) copy-start(f32[9,512]{1,0:T(8,128)} %conv.1) | copy-start | bytes 55300
  1.5 0.8 %copy-start.1 = (bf16[512,32]{0,1:T(8,128)(2,1)S(1)}, bf16[512,32]{0,1:T(8,128)(2,1)}, u32[]{:S(2)}) copy-start(bf16[512,32]{0,1:T(8,128)(2,1)} %param.17) | copy-start | bytes 98308
